TPU v7x, 32 devices: a whole 2x2x4 slice. The times are simulated.
32 devices in a mesh: layer: 8 (over y, x, core), tile: 4 (over z).
Axes of the slice: x: 2, y: 2, z: 4, core: 2. Of those that a mesh axis runs over, the one named last changes fastest.
Arguments:
- incident: bfloat16 [4096, 128], P('tile'), may hold values from -6 to 6
- interface: bfloat16 [16, 4096, 4096], P('layer', 'tile'), may hold values from -0.09375 to 0.09375
- eigvec: bfloat16 [16, 4096, 4096], P('layer', 'tile'), may hold values from -0.09375 to 0.09375
- angle: float32 [16, 4096], P('layer'), may hold values from -3.140625 to 3.140625
- decay: float32 [16, 4096], P('layer'), may hold values from 0.002 to 0.15
Outputs:
- fields: bfloat16 [16, 4096, 512], P('layer', 'tile')
- leaving: float32 [16, 4096, 128], P('layer', 'tile')
All inputs are finite; a program needn't handle non-finite values.
Results may differ from a plain program's by a relative error of at most 0.035.
Values sent between devices are 32-bit elements; how exact they have to be, the bound alone decides.
A program may use at most 128 MiB of HBM per device.

v0:
```python
import jax
import jax.numpy as jnp
from jax import lax
from jax.sharding import PartitionSpec as P

DEPTHS = 4


def shifted(x, axis, by):
    peers = lax.axis_size(axis)
    pairs = [(i, i + by) for i in range(peers) if 0 <= i + by < peers]
    return lax.ppermute(x, axis, pairs)


def rotate(block, angle_row, decay_row, frac):
    half = block.shape[1] // 2
    real_part = block[:, :half]
    imag_part = block[:, half:]
    scale = jnp.exp(-frac * decay_row)
    cosine = (scale * jnp.cos(frac * angle_row))[:, None]
    sine = (scale * jnp.sin(frac * angle_row))[:, None]
    return jnp.concatenate(
        [cosine * real_part - sine * imag_part, sine * real_part + cosine * imag_part], axis=1
    )


def advance(current, interface, angle, decay):
    fulls = []
    leaves = []
    for layer_num in range(interface.shape[0]):
        full = lax.all_gather(current, "tile", axis=0, tiled=True)
        fulls.append(full)
        phased = rotate(full, angle[layer_num], decay[layer_num], 1.0).astype(jnp.bfloat16)
        current = jnp.dot(interface[layer_num], phased, preferred_element_type=jnp.float32)
        leaves.append(current)
    return (jnp.stack(fulls), jnp.stack(leaves))


def pick_block(values, block_num, block_width, half):
    real_part = lax.dynamic_slice_in_dim(
        values, block_num * block_width, block_width, values.ndim - 1
    )
    imag_part = lax.dynamic_slice_in_dim(
        values, half + block_num * block_width, block_width, values.ndim - 1
    )
    return jnp.concatenate([real_part, imag_part], axis=values.ndim - 1)


def put_block(values, piece, block_num, block_width, half):
    last = values.ndim - 1
    real_piece = lax.slice_in_dim(piece, 0, block_width, axis=last)
    imag_piece = lax.slice_in_dim(piece, block_width, 2 * block_width, axis=last)
    values = lax.dynamic_update_slice_in_dim(values, real_piece, block_num * block_width, last)
    return lax.dynamic_update_slice_in_dim(values, imag_piece, half + block_num * block_width, last)


def on_device(incident, interface, eigvec, angle, decay):
    groups = lax.axis_size("layer")
    member = lax.axis_index("layer")
    layers_here = interface.shape[0]
    shard_rows = interface.shape[1]
    orders = interface.shape[2]
    width = incident.shape[1]
    half = width // 2
    start_amps = incident.astype(jnp.float32)
    store_full = jnp.zeros((layers_here, orders, width), jnp.float32)
    store_leave = jnp.zeros((layers_here, shard_rows, width), jnp.float32)
    block_count = 4
    block_width = half // block_count
    inbox = jnp.zeros((shard_rows, 2 * block_width), jnp.float32)

    def step_blocks(step, carry):
        inbox, store_full, store_leave = carry
        block_num = step - member
        valid = (block_num >= 0) & (block_num < block_count)
        clipped = jnp.clip(block_num, 0, block_count - 1)
        source = jnp.where(member == 0, pick_block(start_amps, clipped, block_width, half), inbox)
        fulls, leaves = advance(source, interface, angle, decay)
        store_full = jnp.where(
            valid, put_block(store_full, fulls, clipped, block_width, half), store_full
        )
        store_leave = jnp.where(
            valid, put_block(store_leave, leaves, clipped, block_width, half), store_leave
        )
        inbox = shifted(leaves[layers_here - 1], "layer", 1)
        return (inbox, store_full, store_leave)

    inbox, store_full, store_leave = lax.fori_loop(
        0, groups + block_count - 1, step_blocks, (inbox, store_full, store_leave)
    )
    fields = []
    for layer_num in range(layers_here):
        depth = jnp.concatenate(
            [
                rotate(
                    store_full[layer_num], angle[layer_num], decay[layer_num], step / DEPTHS
                ).astype(jnp.bfloat16)
                for step in range(DEPTHS)
            ],
            axis=1,
        )
        fields.append(
            jnp.dot(eigvec[layer_num], depth, preferred_element_type=jnp.float32).astype(
                jnp.bfloat16
            )
        )
    return (jnp.stack(fields), store_leave)


def solution(mesh):
    in_specs = (
        P("tile", None),
        P("layer", "tile", None),
        P("layer", "tile", None),
        P("layer", None),
        P("layer", None),
    )
    out_specs = (P("layer", "tile", None), P("layer", "tile", None))
    return jax.shard_map(
        on_device, mesh=mesh, in_specs=in_specs, out_specs=out_specs, check_vma=False
    )
```

profile of v0, /device:TPU:1, one launch (start us, length us, event | category | flops | bytes accessed | tf_op | source)
XLA Modules:
  0.0 704.2 jit_solution(1159093125117101727)
XLA Ops:
  11.3 665.6 %while.20 = (s32[]{:T(128)}, f32[1024,32]{0,1:T(8,128)S(1)}, f32[2,4096,128]{1,2,0:T(8,128)}, f32[2,1024,128]{1,2,0:T(8,128)S(1)}, f32[2,4096]{1,0:T(2,128)}, /*...) while((s32[]{:T(128)}, f32[1024,32]{0,1:T(8,128)S(1)}, ...), condition=%wide.region_1.2_spmd.clone, body=%wide.region_0.1_spmd.clone.sunk | while | flops 543318016 | bytes 56263120 | solution.py:88
  12.3 15.3 %all_gather.24 = f32[4096,32]{0,1:T(8,128)S(1)} all-gather(f32[1024,32]{0,1:T(8,128)S(1)} %maximum_select_fusion.2), channel_id=1, replica_groups=mesh['layer'=8,'tile'=4] {'tile'}, dimensions={0}, use_global_device_ids=true | all-gather | bytes 655360 | tf_op jit(solution)/shard_map/while/body/eval_jaxpr/all_gather | solution.py:31
  34.4 11.9 %all_gather.25 = f32[4096,32]{0,1:T(8,128)S(1)} all-gather(f32[1024,32]{0,1:T(8,128)S(1)} %bitcast.104), channel_id=1, replica_groups=mesh['layer'=8,'tile'=4] {'tile'}, dimensions={0}, use_global_device_ids=true | all-gather | bytes 655360 | tf_op jit(solution)/shard_map/while/body/eval_jaxpr/all_gather | solution.py:31
  53.0 9.5 %collective-permute-start = (f32[1024,32]{0,1:T(8,128)S(1)}, f32[1024,32]{0,1:T(8,128)S(1)}, u32[]{:S(2)}, u32[]{:S(2)}) collective-permute-start(f32[1024,32]{0,1:T(8,128)S(1)} %bitcast.107), channel_id=1, source_target_pairs={{0,4},{4,8},{8,12},{12,16},{16,20},{20,24},{24,28},{1,5},{5,9},{9,... | collective-permute-start | bytes 393224 | tf_op jit(solution)/shard_map/while/body/eval_jaxpr/ppermute | solution.py:12
  71.0 13.6 %all_gather.24 = f32[4096,32]{0,1:T(8,128)S(1)} all-gather(f32[1024,32]{0,1:T(8,128)S(1)} %maximum_select_fusion.2), channel_id=1, replica_groups=mesh['layer'=8,'tile'=4] {'tile'}, dimensions={0}, use_global_device_ids=true | all-gather | bytes 655360 | tf_op jit(solution)/shard_map/while/body/eval_jaxpr/all_gather | solution.py:31
  91.3 11.9 %all_gather.25 = f32[4096,32]{0,1:T(8,128)S(1)} all-gather(f32[1024,32]{0,1:T(8,128)S(1)} %bitcast.104), channel_id=1, replica_groups=mesh['layer'=8,'tile'=4] {'tile'}, dimensions={0}, use_global_device_ids=true | all-gather | bytes 655360 | tf_op jit(solution)/shard_map/while/body/eval_jaxpr/all_gather | solution.py:31
  109.9 8.0 %collective-permute-start = (f32[1024,32]{0,1:T(8,128)S(1)}, f32[1024,32]{0,1:T(8,128)S(1)}, u32[]{:S(2)}, u32[]{:S(2)}) collective-permute-start(f32[1024,32]{0,1:T(8,128)S(1)} %bitcast.107), channel_id=1, source_target_pairs={{0,4},{4,8},{8,12},{12,16},{16,20},{20,24},{24,28},{1,5},{5,9},{9,... | collective-permute-start | bytes 393224 | tf_op jit(solution)/shard_map/while/body/eval_jaxpr/ppermute | solution.py:12
  132.1 14.9 %all_gather.24 = f32[4096,32]{0,1:T(8,128)S(1)} all-gather(f32[1024,32]{0,1:T(8,128)S(1)} %maximum_select_fusion.2), channel_id=1, replica_groups=mesh['layer'=8,'tile'=4] {'tile'}, dimensions={0}, use_global_device_ids=true | all-gather | bytes 655360 | tf_op jit(solution)/shard_map/while/body/eval_jaxpr/all_gather | solution.py:31
  153.7 14.3 %all_gather.25 = f32[4096,32]{0,1:T(8,128)S(1)} all-gather(f32[1024,32]{0,1:T(8,128)S(1)} %bitcast.104), channel_id=1, replica_groups=mesh['layer'=8,'tile'=4] {'tile'}, dimensions={0}, use_global_device_ids=true | all-gather | bytes 655360 | tf_op jit(solution)/shard_map/while/body/eval_jaxpr/all_gather | solution.py:31
  193.1 15.5 %all_gather.24 = f32[4096,32]{0,1:T(8,128)S(1)} all-gather(f32[1024,32]{0,1:T(8,128)S(1)} %maximum_select_fusion.2), channel_id=1, replica_groups=mesh['layer'=8,'tile'=4] {'tile'}, dimensions={0}, use_global_device_ids=true | all-gather | bytes 655360 | tf_op jit(solution)/shard_map/while/body/eval_jaxpr/all_gather | solution.py:31
  215.4 13.9 %all_gather.25 = f32[4096,32]{0,1:T(8,128)S(1)} all-gather(f32[1024,32]{0,1:T(8,128)S(1)} %bitcast.104), channel_id=1, replica_groups=mesh['layer'=8,'tile'=4] {'tile'}, dimensions={0}, use_global_device_ids=true | all-gather | bytes 655360 | tf_op jit(solution)/shard_map/while/body/eval_jaxpr/all_gather | solution.py:31
  255.2 14.3 %all_gather.24 = f32[4096,32]{0,1:T(8,128)S(1)} all-gather(f32[1024,32]{0,1:T(8,128)S(1)} %maximum_select_fusion.2), channel_id=1, replica_groups=mesh['layer'=8,'tile'=4] {'tile'}, dimensions={0}, use_global_device_ids=true | all-gather | bytes 655360 | tf_op jit(solution)/shard_map/while/body/eval_jaxpr/all_gather | solution.py:31
  276.2 13.6 %all_gather.25 = f32[4096,32]{0,1:T(8,128)S(1)} all-gather(f32[1024,32]{0,1:T(8,128)S(1)} %bitcast.104), channel_id=1, replica_groups=mesh['layer'=8,'tile'=4] {'tile'}, dimensions={0}, use_global_device_ids=true | all-gather | bytes 655360 | tf_op jit(solution)/shard_map/while/body/eval_jaxpr/all_gather | solution.py:31
  316.4 14.3 %all_gather.24 = f32[4096,32]{0,1:T(8,128)S(1)} all-gather(f32[1024,32]{0,1:T(8,128)S(1)} %maximum_select_fusion.2), channel_id=1, replica_groups=mesh['layer'=8,'tile'=4] {'tile'}, dimensions={0}, use_global_device_ids=true | all-gather | bytes 655360 | tf_op jit(solution)/shard_map/while/body/eval_jaxpr/all_gather | solution.py:31
  337.4 13.9 %all_gather.25 = f32[4096,32]{0,1:T(8,128)S(1)} all-gather(f32[1024,32]{0,1:T(8,128)S(1)} %bitcast.104), channel_id=1, replica_groups=mesh['layer'=8,'tile'=4] {'tile'}, dimensions={0}, use_global_device_ids=true | all-gather | bytes 655360 | tf_op jit(solution)/shard_map/while/body/eval_jaxpr/all_gather | solution.py:31
  376.7 13.5 %all_gather.24 = f32[4096,32]{0,1:T(8,128)S(1)} all-gather(f32[1024,32]{0,1:T(8,128)S(1)} %maximum_select_fusion.2), channel_id=1, replica_groups=mesh['layer'=8,'tile'=4] {'tile'}, dimensions={0}, use_global_device_ids=true | all-gather | bytes 655360 | tf_op jit(solution)/shard_map/while/body/eval_jaxpr/all_gather | solution.py:31
  397.0 13.6 %all_gather.25 = f32[4096,32]{0,1:T(8,128)S(1)} all-gather(f32[1024,32]{0,1:T(8,128)S(1)} %bitcast.104), channel_id=1, replica_groups=mesh['layer'=8,'tile'=4] {'tile'}, dimensions={0}, use_global_device_ids=true | all-gather | bytes 655360 | tf_op jit(solution)/shard_map/while/body/eval_jaxpr/all_gather | solution.py:31
  417.3 7.9 %collective-permute-start = (f32[1024,32]{0,1:T(8,128)S(1)}, f32[1024,32]{0,1:T(8,128)S(1)}, u32[]{:S(2)}, u32[]{:S(2)}) collective-permute-start(f32[1024,32]{0,1:T(8,128)S(1)} %bitcast.107), channel_id=1, source_target_pairs={{0,4},{4,8},{8,12},{12,16},{16,20},{20,24},{24,28},{1,5},{5,9},{9,... | collective-permute-start | bytes 393224 | tf_op jit(solution)/shard_map/while/body/eval_jaxpr/ppermute | solution.py:12
  438.2 12.0 %all_gather.24 = f32[4096,32]{0,1:T(8,128)S(1)} all-gather(f32[1024,32]{0,1:T(8,128)S(1)} %maximum_select_fusion.2), channel_id=1, replica_groups=mesh['layer'=8,'tile'=4] {'tile'}, dimensions={0}, use_global_device_ids=true | all-gather | bytes 655360 | tf_op jit(solution)/shard_map/while/body/eval_jaxpr/all_gather | solution.py:31
  456.9 14.2 %all_gather.25 = f32[4096,32]{0,1:T(8,128)S(1)} all-gather(f32[1024,32]{0,1:T(8,128)S(1)} %bitcast.104), channel_id=1, replica_groups=mesh['layer'=8,'tile'=4] {'tile'}, dimensions={0}, use_global_device_ids=true | all-gather | bytes 655360 | tf_op jit(solution)/shard_map/while/body/eval_jaxpr/all_gather | solution.py:31
  477.9 7.3 %collective-permute-start = (f32[1024,32]{0,1:T(8,128)S(1)}, f32[1024,32]{0,1:T(8,128)S(1)}, u32[]{:S(2)}, u32[]{:S(2)}) collective-permute-start(f32[1024,32]{0,1:T(8,128)S(1)} %bitcast.107), channel_id=1, source_target_pairs={{0,4},{4,8},{8,12},{12,16},{16,20},{20,24},{24,28},{1,5},{5,9},{9,... | collective-permute-start | bytes 393224 | tf_op jit(solution)/shard_map/while/body/eval_jaxpr/ppermute | solution.py:12
  498.2 12.1 %all_gather.24 = f32[4096,32]{0,1:T(8,128)S(1)} all-gather(f32[1024,32]{0,1:T(8,128)S(1)} %maximum_select_fusion.2), channel_id=1, replica_groups=mesh['layer'=8,'tile'=4] {'tile'}, dimensions={0}, use_global_device_ids=true | all-gather | bytes 655360 | tf_op jit(solution)/shard_map/while/body/eval_jaxpr/all_gather | solution.py:31
  517.0 14.0 %all_gather.25 = f32[4096,32]{0,1:T(8,128)S(1)} all-gather(f32[1024,32]{0,1:T(8,128)S(1)} %bitcast.104), channel_id=1, replica_groups=mesh['layer'=8,'tile'=4] {'tile'}, dimensions={0}, use_global_device_ids=true | all-gather | bytes 655360 | tf_op jit(solution)/shard_map/while/body/eval_jaxpr/all_gather | solution.py:31
  537.8 7.2 %collective-permute-start = (f32[1024,32]{0,1:T(8,128)S(1)}, f32[1024,32]{0,1:T(8,128)S(1)}, u32[]{:S(2)}, u32[]{:S(2)}) collective-permute-start(f32[1024,32]{0,1:T(8,128)S(1)} %bitcast.107), channel_id=1, source_target_pairs={{0,4},{4,8},{8,12},{12,16},{16,20},{20,24},{24,28},{1,5},{5,9},{9,... | collective-permute-start | bytes 393224 | tf_op jit(solution)/shard_map/while/body/eval_jaxpr/ppermute | solution.py:12
  558.0 12.3 %all_gather.24 = f32[4096,32]{0,1:T(8,128)S(1)} all-gather(f32[1024,32]{0,1:T(8,128)S(1)} %maximum_select_fusion.2), channel_id=1, replica_groups=mesh['layer'=8,'tile'=4] {'tile'}, dimensions={0}, use_global_device_ids=true | all-gather | bytes 655360 | tf_op jit(solution)/shard_map/while/body/eval_jaxpr/all_gather | solution.py:31
  577.1 13.9 %all_gather.25 = f32[4096,32]{0,1:T(8,128)S(1)} all-gather(f32[1024,32]{0,1:T(8,128)S(1)} %bitcast.104), channel_id=1, replica_groups=mesh['layer'=8,'tile'=4] {'tile'}, dimensions={0}, use_global_device_ids=true | all-gather | bytes 655360 | tf_op jit(solution)/shard_map/while/body/eval_jaxpr/all_gather | solution.py:31
  597.8 7.2 %collective-permute-start = (f32[1024,32]{0,1:T(8,128)S(1)}, f32[1024,32]{0,1:T(8,128)S(1)}, u32[]{:S(2)}, u32[]{:S(2)}) collective-permute-start(f32[1024,32]{0,1:T(8,128)S(1)} %bitcast.107), channel_id=1, source_target_pairs={{0,4},{4,8},{8,12},{12,16},{16,20},{20,24},{24,28},{1,5},{5,9},{9,... | collective-permute-start | bytes 393224 | tf_op jit(solution)/shard_map/while/body/eval_jaxpr/ppermute | solution.py:12
  617.9 12.3 %all_gather.24 = f32[4096,32]{0,1:T(8,128)S(1)} all-gather(f32[1024,32]{0,1:T(8,128)S(1)} %maximum_select_fusion.2), channel_id=1, replica_groups=mesh['layer'=8,'tile'=4] {'tile'}, dimensions={0}, use_global_device_ids=true | all-gather | bytes 655360 | tf_op jit(solution)/shard_map/while/body/eval_jaxpr/all_gather | solution.py:31
  636.9 14.3 %all_gather.25 = f32[4096,32]{0,1:T(8,128)S(1)} all-gather(f32[1024,32]{0,1:T(8,128)S(1)} %bitcast.104), channel_id=1, replica_groups=mesh['layer'=8,'tile'=4] {'tile'}, dimensions={0}, use_global_device_ids=true | all-gather | bytes 655360 | tf_op jit(solution)/shard_map/while/body/eval_jaxpr/all_gather | solution.py:31
  658.0 6.9 collective-permute-start
  685.7 7.3 %fusion.35 = bf16[1,1024,512]{1,2,0:T(8,128)(2,1)S(1)} fusion(bf16[4096,512]{0,1:T(8,128)(2,1)S(1)} %fusion.45, bf16[2,1024,4096]{2,1,0:T(8,128)(2,1)} %param.9), kind=kOutput, calls=%fused_computation.51 | convolution fusion | flops 4295491584 | bytes 13631488 | tf_op jit(solution)/shard_map/dot_general | solution.py:103
  694.4 7.1 %fusion.32 = bf16[1,1024,512]{1,2,0:T(8,128)(2,1)S(1)} fusion(bf16[4096,512]{0,1:T(8,128)(2,1)S(1)} %fusion.53, bf16[2,1024,4096]{2,1,0:T(8,128)(2,1)} %param.9), kind=kOutput, calls=%fused_computation.50 | convolution fusion | flops 4295491584 | bytes 13631488 | tf_op jit(solution)/shard_map/dot_general | solution.py:103
  (306 shorter events, 333.8 us)
Async XLA Ops:
  11.3 1.0 copy-start.1
  53.0 16.9 %collective-permute-start = (f32[1024,32]{0,1:T(8,128)S(1)}, f32[1024,32]{0,1:T(8,128)S(1)}, u32[]{:S(2)}, u32[]{:S(2)}) collective-permute-start(f32[1024,32]{0,1:T(8,128)S(1)} %bitcast.107), channel_id=1, source_target_pairs={{0,4},{4,8},{8,12},{12,16},{16,20},{20,24},{24,28},{1,5},{5,9},{9,... | collective-permute-start | bytes 393224 | tf_op jit(solution)/shard_map/while/body/eval_jaxpr/ppermute | solution.py:12
  66.8 3.1 copy-start.2
  109.9 21.1 %collective-permute-start = (f32[1024,32]{0,1:T(8,128)S(1)}, f32[1024,32]{0,1:T(8,128)S(1)}, u32[]{:S(2)}, u32[]{:S(2)}) collective-permute-start(f32[1024,32]{0,1:T(8,128)S(1)} %bitcast.107), channel_id=1, source_target_pairs={{0,4},{4,8},{8,12},{12,16},{16,20},{20,24},{24,28},{1,5},{5,9},{9,... | collective-permute-start | bytes 393224 | tf_op jit(solution)/shard_map/while/body/eval_jaxpr/ppermute | solution.py:12
  124.4 6.6 copy-start.2
  174.8 17.3 %collective-permute-start = (f32[1024,32]{0,1:T(8,128)S(1)}, f32[1024,32]{0,1:T(8,128)S(1)}, u32[]{:S(2)}, u32[]{:S(2)}) collective-permute-start(f32[1024,32]{0,1:T(8,128)S(1)} %bitcast.107), channel_id=1, source_target_pairs={{0,4},{4,8},{8,12},{12,16},{16,20},{20,24},{24,28},{1,5},{5,9},{9,... | collective-permute-start | bytes 393224 | tf_op jit(solution)/shard_map/while/body/eval_jaxpr/ppermute | solution.py:12
  185.5 6.6 copy-start.2
  236.1 18.1 %collective-permute-start = (f32[1024,32]{0,1:T(8,128)S(1)}, f32[1024,32]{0,1:T(8,128)S(1)}, u32[]{:S(2)}, u32[]{:S(2)}) collective-permute-start(f32[1024,32]{0,1:T(8,128)S(1)} %bitcast.107), channel_id=1, source_target_pairs={{0,4},{4,8},{8,12},{12,16},{16,20},{20,24},{24,28},{1,5},{5,9},{9,... | collective-permute-start | bytes 393224 | tf_op jit(solution)/shard_map/while/body/eval_jaxpr/ppermute | solution.py:12
  247.6 6.6 copy-start.2
  296.6 18.7 %collective-permute-start = (f32[1024,32]{0,1:T(8,128)S(1)}, f32[1024,32]{0,1:T(8,128)S(1)}, u32[]{:S(2)}, u32[]{:S(2)}) collective-permute-start(f32[1024,32]{0,1:T(8,128)S(1)} %bitcast.107), channel_id=1, source_target_pairs={{0,4},{4,8},{8,12},{12,16},{16,20},{20,24},{24,28},{1,5},{5,9},{9,... | collective-permute-start | bytes 393224 | tf_op jit(solution)/shard_map/while/body/eval_jaxpr/ppermute | solution.py:12
  308.7 6.6 copy-start.2
  358.0 17.6 %collective-permute-start = (f32[1024,32]{0,1:T(8,128)S(1)}, f32[1024,32]{0,1:T(8,128)S(1)}, u32[]{:S(2)}, u32[]{:S(2)}) collective-permute-start(f32[1024,32]{0,1:T(8,128)S(1)} %bitcast.107), channel_id=1, source_target_pairs={{0,4},{4,8},{8,12},{12,16},{16,20},{20,24},{24,28},{1,5},{5,9},{9,... | collective-permute-start | bytes 393224 | tf_op jit(solution)/shard_map/while/body/eval_jaxpr/ppermute | solution.py:12
  370.3 5.3 copy-start.2
  417.3 19.8 %collective-permute-start = (f32[1024,32]{0,1:T(8,128)S(1)}, f32[1024,32]{0,1:T(8,128)S(1)}, u32[]{:S(2)}, u32[]{:S(2)}) collective-permute-start(f32[1024,32]{0,1:T(8,128)S(1)} %bitcast.107), channel_id=1, source_target_pairs={{0,4},{4,8},{8,12},{12,16},{16,20},{20,24},{24,28},{1,5},{5,9},{9,... | collective-permute-start | bytes 393224 | tf_op jit(solution)/shard_map/while/body/eval_jaxpr/ppermute | solution.py:12
  431.8 5.3 copy-start.2
  477.9 19.2 %collective-permute-start = (f32[1024,32]{0,1:T(8,128)S(1)}, f32[1024,32]{0,1:T(8,128)S(1)}, u32[]{:S(2)}, u32[]{:S(2)}) collective-permute-start(f32[1024,32]{0,1:T(8,128)S(1)} %bitcast.107), channel_id=1, source_target_pairs={{0,4},{4,8},{8,12},{12,16},{16,20},{20,24},{24,28},{1,5},{5,9},{9,... | collective-permute-start | bytes 393224 | tf_op jit(solution)/shard_map/while/body/eval_jaxpr/ppermute | solution.py:12
  491.8 5.3 copy-start.2
  537.8 19.1 %collective-permute-start = (f32[1024,32]{0,1:T(8,128)S(1)}, f32[1024,32]{0,1:T(8,128)S(1)}, u32[]{:S(2)}, u32[]{:S(2)}) collective-permute-start(f32[1024,32]{0,1:T(8,128)S(1)} %bitcast.107), channel_id=1, source_target_pairs={{0,4},{4,8},{8,12},{12,16},{16,20},{20,24},{24,28},{1,5},{5,9},{9,... | collective-permute-start | bytes 393224 | tf_op jit(solution)/shard_map/while/body/eval_jaxpr/ppermute | solution.py:12
  551.6 5.3 copy-start.2
  597.8 19.1 %collective-permute-start = (f32[1024,32]{0,1:T(8,128)S(1)}, f32[1024,32]{0,1:T(8,128)S(1)}, u32[]{:S(2)}, u32[]{:S(2)}) collective-permute-start(f32[1024,32]{0,1:T(8,128)S(1)} %bitcast.107), channel_id=1, source_target_pairs={{0,4},{4,8},{8,12},{12,16},{16,20},{20,24},{24,28},{1,5},{5,9},{9,... | collective-permute-start | bytes 393224 | tf_op jit(solution)/shard_map/while/body/eval_jaxpr/ppermute | solution.py:12
  611.6 5.3 copy-start.2
  658.0 18.9 %collective-permute-start = (f32[1024,32]{0,1:T(8,128)S(1)}, f32[1024,32]{0,1:T(8,128)S(1)}, u32[]{:S(2)}, u32[]{:S(2)}) collective-permute-start(f32[1024,32]{0,1:T(8,128)S(1)} %bitcast.107), channel_id=1, source_target_pairs={{0,4},{4,8},{8,12},{12,16},{16,20},{20,24},{24,28},{1,5},{5,9},{9,... | collective-permute-start | bytes 393224 | tf_op jit(solution)/shard_map/while/body/eval_jaxpr/ppermute | solution.py:12
  671.5 5.3 copy-start.2
  676.9 5.3 copy-start.15
  676.9 5.3 copy-start.16
  676.9 5.3 copy-start.17
  676.9 5.3 copy-start.18
  682.2 2.2 copy-start
  682.2 2.4 copy-start.13
  682.2 2.4 copy-start.14
  685.7 7.5 %copy-start.4 = (f32[1,4096]{1,0:T(1,128)S(1)}, f32[1,4096]{1,0:T(1,128)}, u32[]{:S(2)}) copy-start(f32[1,4096]{1,0:T(1,128)} %get-tuple-element.339) | copy-start | bytes 49156
  685.7 7.5 %copy-start.8 = (f32[1,4096]{1,0:T(1,128)S(1)}, f32[1,4096]{1,0:T(1,128)}, u32[]{:S(2)}) copy-start(f32[1,4096]{1,0:T(1,128)} %get-tuple-element.344) | copy-start | bytes 49156
  (18 other events, 15.7 us)
where the time goes:
time: 709 us; the launch traced here: 704 us
  blocking collectives  300 us (42%)
  other arithmetic  173 us (24%)
  matrix products  145 us (20%)
  starting transfers between devices  74.1 us (10%)
  local copies, waits for them, and re-layouts  9.94 us (1%)
    all_gather x22, blocking collectives, advance(): full = lax.all_gather(current, 'tile', axis=0, tiled=True)  300 us
    dot_general x22, matrix products, advance(): jnp.dot(interface[layer_num], phased, preferred_element_type=jnp.float32)  131 us
    ppermute x11, starting transfers between devices, shifted(): return lax.ppermute(x, axis, pairs)  74.1 us
    select_n x11, other arithmetic, step_blocks(): jnp.where(valid, put_block(store_full, fulls, clipped, block_width, half)...  57.7 us
    while x22, other arithmetic  50.2 us
    mul x24, other arithmetic, rotate(): cosine = (scale * jnp.cos(frac * angle_row))[:, None]  25.5 us
    dot_general x2, matrix products, on_device(): jnp.dot(eigvec[layer_num], depth, preferred_element_type=jnp.float32)  14.4 us
  transfers between devices with their start and end apart: 11, of which 0 were waited for; matrix products, arithmetic and copies ran while one was open for 19% of the time, Pallas kernels for 0%

commit v1 on v0

--- a/solution.py
+++ b/solution.py
@@ -1,9 +1,26 @@
+import functools
 import jax
 import jax.numpy as jnp
 from jax import lax
 from jax.sharding import PartitionSpec as P
 
 DEPTHS = 4
+
+
+def draft_matrix(panel, dev_axis):
+    n_shards = lax.axis_size(dev_axis)
+    by_place = tuple(((ii, (ii + 1) % n_shards) for ii in range(n_shards)))
+    e_now = [None] * n_shards
+    e_now[n_shards - 1] = panel
+    for h in range(n_shards - 2, -1, -1):
+        e_now[h] = lax.ppermute(e_now[h + 1], axis_name=dev_axis, perm=by_place)
+    placed = jnp.concatenate(e_now, 0)
+    mixed_arr = (lax.axis_index(dev_axis) + 1) * panel.shape[0]
+    newest = jnp.roll(placed, mixed_arr, axis=0)
+    return newest
+
+
+lines_clear = functools.partial(draft_matrix, dev_axis="tile")
 
 
 def shifted(x, axis, by):
@@ -28,7 +45,7 @@
     fulls = []
     leaves = []
     for layer_num in range(interface.shape[0]):
-        full = lax.all_gather(current, "tile", axis=0, tiled=True)
+        full = lines_clear(current)
         fulls.append(full)
         phased = rotate(full, angle[layer_num], decay[layer_num], 1.0).astype(jnp.bfloat16)
         current = jnp.dot(interface[layer_num], phased, preferred_element_type=jnp.float32)

time: 709 us -> 724 us (1.021)
  waiting for transfers between devices: 0.03 us -> 355 us
  blocking collectives: 300 us -> 0 us
  other arithmetic: 173 us -> 78.5 us
  starting transfers between devices: 74.1 us -> 107 us
  local copies, waits for them, and re-layouts: 9.94 us -> 26 us
    ppermute x0 -> x66, waiting for transfers between devices: none -> 354 us  [draft_matrix(): e_now[h] = lax.ppermute(e_now[h + 1], axis_name=dev_axis, perm=by_place)]
    all_gather x22 -> x0, blocking collectives: 300 us -> none  [advance(): full = lax.all_gather(current, 'tile', axis=0, tiled=True)]
    select_n x11, other arithmetic: 57.7 us -> 13.9 us  [step_blocks(): jnp.where(valid, put_block(store_full, fulls, clipped, block_width, half)...]
    ppermute x11, starting transfers between devices: 74.1 us -> 104 us  [shifted(): return lax.ppermute(x, axis, pairs)]
    while x22, other arithmetic: 50.2 us -> 28 us
    mul x24, other arithmetic: 25.5 us -> 8.21 us  [rotate(): cosine = (scale * jnp.cos(frac * angle_row))[:, None]]
    while x44 -> x132, local copies, waits for them, and re-layouts: 0.11 us -> 16.8 us
    dynamic_update_slice x22, other arithmetic: 9.93 us -> 0.86 us  [put_block(): lax.dynamic_update_slice_in_dim(values, imag_piece, half + block_num * bl...]
  transfers between devices with their start and end apart: 11 -> 77, of which waited for: 0 -> 77; matrix products, arithmetic and copies ran while one was open for 19% -> 8% of each run, Pallas kernels for 0% -> 0%
where the time goes in v1:
time: 724 us; the launch traced here: 718 us
  waiting for transfers between devices  355 us (49%)
  matrix products  149 us (21%)
  starting transfers between devices  107 us (15%)
  other arithmetic  78.5 us (11%)
  local copies, waits for them, and re-layouts  26 us (4%)
    ppermute x66, waiting for transfers between devices, draft_matrix(): e_now[h] = lax.ppermute(e_now[h + 1], axis_name=dev_axis, perm=by_place)  354 us
    dot_general x22, matrix products, advance(): jnp.dot(interface[layer_num], phased, preferred_element_type=jnp.float32)  134 us
    ppermute x11, starting transfers between devices, shifted(): return lax.ppermute(x, axis, pairs)  104 us
    while x22, other arithmetic  28 us
    while x132, local copies, waits for them, and re-layouts  16.8 us
  transfers between devices with their start and end apart: 77, of which 77 were waited for; matrix products, arithmetic and copies ran while one was open for 8% of the time, Pallas kernels for 0%

profile of v1, /device:TPU:1, one launch (start us, length us, event | category | flops | bytes accessed | tf_op | source)
XLA Modules:
  0.0 718.2 jit_solution(16173596345799544350)
XLA Ops:
  9.9 681.7 %while.20 = (s32[]{:T(128)}, f32[1024,32]{0,1:T(8,128)S(1)}, f32[2,4096,128]{1,2,0:T(8,128)}, f32[2,1024,128]{1,2,0:T(8,128)S(1)}, f32[2,4096]{1,0:T(2,128)}, /*...) while((s32[]{:T(128)}, f32[1024,32]{0,1:T(8,128)S(1)}, ...), condition=%wide.region_1.3_spmd.clone, body=%wide.region_0.2_spmd.clone.sunk | while | flops 545153024 | bytes 127304736 | solution.py:105
  46.4 6.6 collective-permute-done.5
  59.5 10.2 %collective-permute-start.6 = (f32[1024,32]{0,1:T(8,128)S(1)}, f32[1024,32]{0,1:T(8,128)S(1)}, u32[]{:S(2)}, u32[]{:S(2)}) collective-permute-start(f32[1024,32]{0,1:T(8,128)S(1)} %bitcast.108), channel_id=1, source_target_pairs={{0,4},{4,8},{8,12},{12,16},{16,20},{20,24},{24,28},{1,5},{5,9},{9,... | collective-permute-start | bytes 393224 | tf_op jit(solution)/shard_map/while/body/eval_jaxpr/ppermute | solution.py:29
  85.6 6.5 collective-permute-done.2
  122.0 9.2 %collective-permute-start.6 = (f32[1024,32]{0,1:T(8,128)S(1)}, f32[1024,32]{0,1:T(8,128)S(1)}, u32[]{:S(2)}, u32[]{:S(2)}) collective-permute-start(f32[1024,32]{0,1:T(8,128)S(1)} %bitcast.108), channel_id=1, source_target_pairs={{0,4},{4,8},{8,12},{12,16},{16,20},{20,24},{24,28},{1,5},{5,9},{9,... | collective-permute-start | bytes 393224 | tf_op jit(solution)/shard_map/while/body/eval_jaxpr/ppermute | solution.py:29
  146.1 6.5 collective-permute-done.2
  183.6 9.7 %collective-permute-start.6 = (f32[1024,32]{0,1:T(8,128)S(1)}, f32[1024,32]{0,1:T(8,128)S(1)}, u32[]{:S(2)}, u32[]{:S(2)}) collective-permute-start(f32[1024,32]{0,1:T(8,128)S(1)} %bitcast.108), channel_id=1, source_target_pairs={{0,4},{4,8},{8,12},{12,16},{16,20},{20,24},{24,28},{1,5},{5,9},{9,... | collective-permute-start | bytes 393224 | tf_op jit(solution)/shard_map/while/body/eval_jaxpr/ppermute | solution.py:29
  226.2 7.2 collective-permute-done.4
  233.4 6.4 collective-permute-done.5
  240.2 6.1 fusion.95
  246.3 8.7 %collective-permute-start.6 = (f32[1024,32]{0,1:T(8,128)S(1)}, f32[1024,32]{0,1:T(8,128)S(1)}, u32[]{:S(2)}, u32[]{:S(2)}) collective-permute-start(f32[1024,32]{0,1:T(8,128)S(1)} %bitcast.108), channel_id=1, source_target_pairs={{0,4},{4,8},{8,12},{12,16},{16,20},{20,24},{24,28},{1,5},{5,9},{9,... | collective-permute-start | bytes 393224 | tf_op jit(solution)/shard_map/while/body/eval_jaxpr/ppermute | solution.py:29
  258.5 6.1 collective-permute-done
  293.8 7.0 collective-permute-done.5
  307.3 9.4 %collective-permute-start.6 = (f32[1024,32]{0,1:T(8,128)S(1)}, f32[1024,32]{0,1:T(8,128)S(1)}, u32[]{:S(2)}, u32[]{:S(2)}) collective-permute-start(f32[1024,32]{0,1:T(8,128)S(1)} %bitcast.108), channel_id=1, source_target_pairs={{0,4},{4,8},{8,12},{12,16},{16,20},{20,24},{24,28},{1,5},{5,9},{9,... | collective-permute-start | bytes 393224 | tf_op jit(solution)/shard_map/while/body/eval_jaxpr/ppermute | solution.py:29
  320.3 7.1 collective-permute-done
  369.1 9.3 %collective-permute-start.6 = (f32[1024,32]{0,1:T(8,128)S(1)}, f32[1024,32]{0,1:T(8,128)S(1)}, u32[]{:S(2)}, u32[]{:S(2)}) collective-permute-start(f32[1024,32]{0,1:T(8,128)S(1)} %bitcast.108), channel_id=1, source_target_pairs={{0,4},{4,8},{8,12},{12,16},{16,20},{20,24},{24,28},{1,5},{5,9},{9,... | collective-permute-start | bytes 393224 | tf_op jit(solution)/shard_map/while/body/eval_jaxpr/ppermute | solution.py:29
  382.0 7.0 collective-permute-done
  424.7 6.1 fusion.95
  430.8 9.4 %collective-permute-start.6 = (f32[1024,32]{0,1:T(8,128)S(1)}, f32[1024,32]{0,1:T(8,128)S(1)}, u32[]{:S(2)}, u32[]{:S(2)}) collective-permute-start(f32[1024,32]{0,1:T(8,128)S(1)} %bitcast.108), channel_id=1, source_target_pairs={{0,4},{4,8},{8,12},{12,16},{16,20},{20,24},{24,28},{1,5},{5,9},{9,... | collective-permute-start | bytes 393224 | tf_op jit(solution)/shard_map/while/body/eval_jaxpr/ppermute | solution.py:29
  443.8 7.1 collective-permute-done
  486.6 6.1 fusion.95
  492.7 9.8 %collective-permute-start.6 = (f32[1024,32]{0,1:T(8,128)S(1)}, f32[1024,32]{0,1:T(8,128)S(1)}, u32[]{:S(2)}, u32[]{:S(2)}) collective-permute-start(f32[1024,32]{0,1:T(8,128)S(1)} %bitcast.108), channel_id=1, source_target_pairs={{0,4},{4,8},{8,12},{12,16},{16,20},{20,24},{24,28},{1,5},{5,9},{9,... | collective-permute-start | bytes 393224 | tf_op jit(solution)/shard_map/while/body/eval_jaxpr/ppermute | solution.py:29
  506.0 7.0 collective-permute-done
  555.0 9.2 %collective-permute-start.6 = (f32[1024,32]{0,1:T(8,128)S(1)}, f32[1024,32]{0,1:T(8,128)S(1)}, u32[]{:S(2)}, u32[]{:S(2)}) collective-permute-start(f32[1024,32]{0,1:T(8,128)S(1)} %bitcast.108), channel_id=1, source_target_pairs={{0,4},{4,8},{8,12},{12,16},{16,20},{20,24},{24,28},{1,5},{5,9},{9,... | collective-permute-start | bytes 393224 | tf_op jit(solution)/shard_map/while/body/eval_jaxpr/ppermute | solution.py:29
  567.8 6.9 collective-permute-done
  610.3 6.1 fusion.95
  616.4 9.8 %collective-permute-start.6 = (f32[1024,32]{0,1:T(8,128)S(1)}, f32[1024,32]{0,1:T(8,128)S(1)}, u32[]{:S(2)}, u32[]{:S(2)}) collective-permute-start(f32[1024,32]{0,1:T(8,128)S(1)} %bitcast.108), channel_id=1, source_target_pairs={{0,4},{4,8},{8,12},{12,16},{16,20},{20,24},{24,28},{1,5},{5,9},{9,... | collective-permute-start | bytes 393224 | tf_op jit(solution)/shard_map/while/body/eval_jaxpr/ppermute | solution.py:29
  629.8 7.1 collective-permute-done
  672.7 6.1 fusion.95
  678.8 9.3 %collective-permute-start.6 = (f32[1024,32]{0,1:T(8,128)S(1)}, f32[1024,32]{0,1:T(8,128)S(1)}, u32[]{:S(2)}, u32[]{:S(2)}) collective-permute-start(f32[1024,32]{0,1:T(8,128)S(1)} %bitcast.108), channel_id=1, source_target_pairs={{0,4},{4,8},{8,12},{12,16},{16,20},{20,24},{24,28},{1,5},{5,9},{9,... | collective-permute-start | bytes 393224 | tf_op jit(solution)/shard_map/while/body/eval_jaxpr/ppermute | solution.py:29
  700.1 7.3 %fusion.49 = bf16[1,1024,512]{1,2,0:T(8,128)(2,1)S(1)} fusion(bf16[4096,512]{0,1:T(8,128)(2,1)S(1)} %fusion.59, bf16[2,1024,4096]{2,1,0:T(8,128)(2,1)} %param.11), kind=kOutput, calls=%fused_computation.81 | convolution fusion | flops 4295491584 | bytes 13631488 | tf_op jit(solution)/shard_map/dot_general | solution.py:120
  708.4 7.1 fusion.46
  (494 shorter events, 477.8 us)
Async XLA Ops:
  10.0 7.4 %collective-permute-start = (f32[1024,32]{0,1:T(8,128)S(1)}, f32[1024,32]{0,1:T(8,128)S(1)}, u32[]{:S(2)}, u32[]{:S(2)}) collective-permute-start(f32[1024,32]{0,1:T(8,128)S(1)} %maximum_select_fusion.2), channel_id=1, source_target_pairs={{0,1},{1,2},{2,3},{3,0},{4,5},{5,6},{6,7},{7,4},{8,9},{9,10},{10,1... | collective-permute-start | bytes 393224 | tf_op jit(solution)/shard_map/while/body/eval_jaxpr/ppermute | solution.py:16
  46.4 6.6 collective-permute-start.5
  59.5 12.2 %collective-permute-start.6 = (f32[1024,32]{0,1:T(8,128)S(1)}, f32[1024,32]{0,1:T(8,128)S(1)}, u32[]{:S(2)}, u32[]{:S(2)}) collective-permute-start(f32[1024,32]{0,1:T(8,128)S(1)} %bitcast.108), channel_id=1, source_target_pairs={{0,4},{4,8},{8,12},{12,16},{16,20},{20,24},{24,28},{1,5},{5,9},{9,... | collective-permute-start | bytes 393224 | tf_op jit(solution)/shard_map/while/body/eval_jaxpr/ppermute | solution.py:29
  78.9 6.7 collective-permute-start.1
  85.6 6.5 collective-permute-start.2
  122.0 11.2 %collective-permute-start.6 = (f32[1024,32]{0,1:T(8,128)S(1)}, f32[1024,32]{0,1:T(8,128)S(1)}, u32[]{:S(2)}, u32[]{:S(2)}) collective-permute-start(f32[1024,32]{0,1:T(8,128)S(1)} %bitcast.108), channel_id=1, source_target_pairs={{0,4},{4,8},{8,12},{12,16},{16,20},{20,24},{24,28},{1,5},{5,9},{9,... | collective-permute-start | bytes 393224 | tf_op jit(solution)/shard_map/while/body/eval_jaxpr/ppermute | solution.py:29
  146.1 6.5 collective-permute-start.2
  159.1 6.7 collective-permute-start.3
  183.6 11.6 %collective-permute-start.6 = (f32[1024,32]{0,1:T(8,128)S(1)}, f32[1024,32]{0,1:T(8,128)S(1)}, u32[]{:S(2)}, u32[]{:S(2)}) collective-permute-start(f32[1024,32]{0,1:T(8,128)S(1)} %bitcast.108), channel_id=1, source_target_pairs={{0,4},{4,8},{8,12},{12,16},{16,20},{20,24},{24,28},{1,5},{5,9},{9,... | collective-permute-start | bytes 393224 | tf_op jit(solution)/shard_map/while/body/eval_jaxpr/ppermute | solution.py:29
  226.1 7.3 %collective-permute-start.4 = (f32[1024,32]{0,1:T(8,128)S(1)}, f32[1024,32]{0,1:T(8,128)S(1)}, u32[]{:S(2)}, u32[]{:S(2)}) collective-permute-start(f32[1024,32]{0,1:T(8,128)S(1)} %collective-permute-done.3), channel_id=1, source_target_pairs={{0,1},{1,2},{2,3},{3,0},{4,5},{5,6},{6,7},{7,4},{8,9},{9,10},{10,1... | collective-permute-start | bytes 393224 | tf_op jit(solution)/shard_map/while/body/eval_jaxpr/ppermute | solution.py:16
  233.3 6.4 collective-permute-start.5
  246.3 10.6 %collective-permute-start.6 = (f32[1024,32]{0,1:T(8,128)S(1)}, f32[1024,32]{0,1:T(8,128)S(1)}, u32[]{:S(2)}, u32[]{:S(2)}) collective-permute-start(f32[1024,32]{0,1:T(8,128)S(1)} %bitcast.108), channel_id=1, source_target_pairs={{0,4},{4,8},{8,12},{12,16},{16,20},{20,24},{24,28},{1,5},{5,9},{9,... | collective-permute-start | bytes 393224 | tf_op jit(solution)/shard_map/while/body/eval_jaxpr/ppermute | solution.py:29
  258.5 6.2 collective-permute-start
  293.8 7.0 collective-permute-start.5
  307.3 11.4 %collective-permute-start.6 = (f32[1024,32]{0,1:T(8,128)S(1)}, f32[1024,32]{0,1:T(8,128)S(1)}, u32[]{:S(2)}, u32[]{:S(2)}) collective-permute-start(f32[1024,32]{0,1:T(8,128)S(1)} %bitcast.108), channel_id=1, source_target_pairs={{0,4},{4,8},{8,12},{12,16},{16,20},{20,24},{24,28},{1,5},{5,9},{9,... | collective-permute-start | bytes 393224 | tf_op jit(solution)/shard_map/while/body/eval_jaxpr/ppermute | solution.py:29
  320.2 7.1 collective-permute-start
  327.3 6.2 collective-permute-start.1
  369.1 11.3 %collective-permute-start.6 = (f32[1024,32]{0,1:T(8,128)S(1)}, f32[1024,32]{0,1:T(8,128)S(1)}, u32[]{:S(2)}, u32[]{:S(2)}) collective-permute-start(f32[1024,32]{0,1:T(8,128)S(1)} %bitcast.108), channel_id=1, source_target_pairs={{0,4},{4,8},{8,12},{12,16},{16,20},{20,24},{24,28},{1,5},{5,9},{9,... | collective-permute-start | bytes 393224 | tf_op jit(solution)/shard_map/while/body/eval_jaxpr/ppermute | solution.py:29
  381.9 7.0 collective-permute-start
  389.0 6.1 collective-permute-start.1
  430.8 11.4 %collective-permute-start.6 = (f32[1024,32]{0,1:T(8,128)S(1)}, f32[1024,32]{0,1:T(8,128)S(1)}, u32[]{:S(2)}, u32[]{:S(2)}) collective-permute-start(f32[1024,32]{0,1:T(8,128)S(1)} %bitcast.108), channel_id=1, source_target_pairs={{0,4},{4,8},{8,12},{12,16},{16,20},{20,24},{24,28},{1,5},{5,9},{9,... | collective-permute-start | bytes 393224 | tf_op jit(solution)/shard_map/while/body/eval_jaxpr/ppermute | solution.py:29
  443.7 7.1 collective-permute-start
  450.9 6.2 collective-permute-start.1
  492.7 11.8 %collective-permute-start.6 = (f32[1024,32]{0,1:T(8,128)S(1)}, f32[1024,32]{0,1:T(8,128)S(1)}, u32[]{:S(2)}, u32[]{:S(2)}) collective-permute-start(f32[1024,32]{0,1:T(8,128)S(1)} %bitcast.108), channel_id=1, source_target_pairs={{0,4},{4,8},{8,12},{12,16},{16,20},{20,24},{24,28},{1,5},{5,9},{9,... | collective-permute-start | bytes 393224 | tf_op jit(solution)/shard_map/while/body/eval_jaxpr/ppermute | solution.py:29
  506.0 7.0 collective-permute-start
  513.0 6.5 collective-permute-start.1
  555.0 11.2 %collective-permute-start.6 = (f32[1024,32]{0,1:T(8,128)S(1)}, f32[1024,32]{0,1:T(8,128)S(1)}, u32[]{:S(2)}, u32[]{:S(2)}) collective-permute-start(f32[1024,32]{0,1:T(8,128)S(1)} %bitcast.108), channel_id=1, source_target_pairs={{0,4},{4,8},{8,12},{12,16},{16,20},{20,24},{24,28},{1,5},{5,9},{9,... | collective-permute-start | bytes 393224 | tf_op jit(solution)/shard_map/while/body/eval_jaxpr/ppermute | solution.py:29
  567.7 6.9 collective-permute-start
  616.4 11.7 %collective-permute-start.6 = (f32[1024,32]{0,1:T(8,128)S(1)}, f32[1024,32]{0,1:T(8,128)S(1)}, u32[]{:S(2)}, u32[]{:S(2)}) collective-permute-start(f32[1024,32]{0,1:T(8,128)S(1)} %bitcast.108), channel_id=1, source_target_pairs={{0,4},{4,8},{8,12},{12,16},{16,20},{20,24},{24,28},{1,5},{5,9},{9,... | collective-permute-start | bytes 393224 | tf_op jit(solution)/shard_map/while/body/eval_jaxpr/ppermute | solution.py:29
  629.7 7.1 collective-permute-start
  636.8 6.5 collective-permute-start.1
  678.8 11.2 %collective-permute-start.6 = (f32[1024,32]{0,1:T(8,128)S(1)}, f32[1024,32]{0,1:T(8,128)S(1)}, u32[]{:S(2)}, u32[]{:S(2)}) collective-permute-start(f32[1024,32]{0,1:T(8,128)S(1)} %bitcast.108), channel_id=1, source_target_pairs={{0,4},{4,8},{8,12},{12,16},{16,20},{20,24},{24,28},{1,5},{5,9},{9,... | collective-permute-start | bytes 393224 | tf_op jit(solution)/shard_map/while/body/eval_jaxpr/ppermute | solution.py:29
  (112 other events, 867.1 us)
